TPU v7x, 32 devices: a whole 2x2x4 slice. The times are simulated.
32 devices in a mesh: pipe: 2 (over x), expert: 16 (over z, y, core).
Axes of the slice: x: 2, y: 2, z: 4, core: 2. Of those that a mesh axis runs over, the one named last changes fastest.
Arguments:
- inputs: bfloat16 [1, 512, 5120], P(None, 'expert'), may hold values from -6 to 6
- router: bfloat16 [2, 5120, 2], P('pipe'), may hold values from -0.078125 to 0.078125
- w_up: bfloat16 [2, 3072, 5120], P('pipe', 'expert'), may hold values from -0.078125 to 0.078125
- w_down: bfloat16 [2, 3072, 5120], P('pipe', 'expert'), may hold values from -0.15625 to 0.15625
- picks: int32 [2, 1, 2, 8], P('pipe'), may hold values from 0 to 511, as said below
- probe: bfloat16 [2, 64, 5120], P('pipe'), may hold values from -0.078125 to 0.078125
Outputs:
- student_feats: bfloat16 [2, 1, 512, 64], P('pipe', None, 'expert')
Inputs may be any that keep to these rules, and one draw needn't show every extreme that they name: Each list picks[s, m, e] holds 8 different token positions of the micro-batch. Of the 32 consecutive positions held by one index of expert, at most 1 stand in one list, and in every list some index has exactly 1.
All inputs are finite; a program needn't handle non-finite values.
Results may differ from a plain program's by a relative error of at most 0.0059.
Values may be sent and summed in bfloat16 or wider, within the bound.
A program may use at most 64 MiB of HBM per device.

v0:
```python
import jax
import jax.numpy as jnp
from jax import lax
from jax.sharding import PartitionSpec as P

SLOT = 1


def passed_along(x, axis, by):
    size = lax.axis_size(axis)
    pairs = [(i, i + by) for i in range(size) if 0 <= i + by < size]
    return lax.ppermute(x, axis, pairs)


def from_root(x, axis, root):
    mine = lax.axis_index(axis) == root
    return lax.psum(jnp.where(mine, x, jnp.zeros_like(x)), axis)


def rms_rows(rows_in):
    wide = rows_in.astype(jnp.float32)
    scale = lax.rsqrt(jnp.mean(wide * wide, axis=-1, keepdims=True) + 1e-06)
    return (wide * scale).astype(jnp.bfloat16)


def shards(inputs, router, w_up, w_down, picks, probe):
    sections = lax.axis_size("pipe")
    expert_width = lax.axis_size("expert")
    section_index = lax.axis_index("pipe")
    source = lax.axis_index("expert")
    micro_count, tok_rows, features = inputs.shape
    experts = router.shape[2]
    group_size = expert_width // experts
    tick_count = micro_count + sections - 1
    positions = jnp.arange(tok_rows, dtype=jnp.int32)
    slot_ids = jnp.arange(SLOT, dtype=jnp.int32)

    def expert_rows(received):
        row_shape = received.shape
        flat_rows = received.reshape(-1, row_shape[2])
        pre = lax.dot_general(
            flat_rows, w_up[0], (((1,), (1,)), ((), ())), preferred_element_type=jnp.float32
        )
        hidden = jax.nn.silu(pre).astype(jnp.bfloat16)
        partials = jnp.dot(hidden, w_down[0], preferred_element_type=jnp.float32).astype(
            jnp.bfloat16
        )
        return partials.reshape(row_shape)

    def layer(rows_in, micro_index):
        normed = rms_rows(rows_in)
        gate_values = jax.nn.sigmoid(jnp.dot(normed, router[0], preferred_element_type=jnp.float32))
        chosen = lax.dynamic_index_in_dim(picks[0], micro_index, 0, keepdims=False)
        local_rows = chosen - source * tok_rows
        owned = (local_rows >= 0) & (local_rows < tok_rows)
        owned_count = owned.astype(jnp.int32)
        slot_place = jnp.cumsum(owned_count, axis=1) - owned_count
        slot_hot = ((slot_place[:, :, None] == slot_ids) & owned[:, :, None]).astype(jnp.bfloat16)
        row_hot = (local_rows[:, :, None] == positions).astype(jnp.bfloat16)
        selector = jnp.einsum("ecr,ect->ert", slot_hot, row_hot, preferred_element_type=jnp.float32)
        picked = jnp.einsum(
            "ert,td->erd", selector.astype(jnp.bfloat16), normed, preferred_element_type=jnp.float32
        ).astype(jnp.bfloat16)
        copies = jnp.repeat(picked, group_size, axis=0)
        partials = expert_rows(
            lax.all_to_all(copies, "expert", split_axis=0, concat_axis=0, tiled=True)
        )
        returned = lax.all_to_all(partials, "expert", split_axis=0, concat_axis=0, tiled=True)
        expert_out = jnp.sum(
            returned.astype(jnp.float32).reshape(experts, group_size, SLOT, features), axis=1
        )
        weights = selector * jnp.transpose(gate_values)[:, None, :]
        update = jnp.einsum("ert,erd->td", weights, expert_out, precision=lax.Precision.HIGHEST)
        return (rows_in.astype(jnp.float32) + update).astype(jnp.bfloat16)

    def tick(tick_index, loop_state):
        previous, finals = loop_state
        arrived = passed_along(previous, "pipe", 1)
        micro_index = jnp.clip(tick_index - section_index, 0, micro_count - 1)
        fresh_rows = lax.dynamic_index_in_dim(
            inputs, jnp.clip(tick_index, 0, micro_count - 1), 0, keepdims=False
        )
        rows_in = jnp.where(section_index == 0, fresh_rows, arrived)
        result = layer(rows_in, micro_index)
        finished = (
            (section_index == sections - 1)
            & (tick_index - section_index >= 0)
            & (tick_index - section_index < micro_count)
        )
        stored = lax.dynamic_update_index_in_dim(finals, result, micro_index, 0)
        finals = jnp.where(finished, stored, finals)
        return (result, finals)

    start_rows = jnp.zeros((tok_rows, features), jnp.bfloat16)
    start_finals = jnp.zeros((micro_count, tok_rows, features), jnp.bfloat16)
    previous, finals = lax.fori_loop(0, tick_count, tick, (start_rows, start_finals))
    shared = from_root(finals, "pipe", sections - 1)
    final_normed = rms_rows(shared)
    student_rows = jnp.einsum(
        "mtd,jd->mtj", final_normed, probe[0], preferred_element_type=jnp.float32
    )
    return student_rows.astype(jnp.bfloat16)[None]


def solution(mesh):
    return jax.shard_map(
        shards,
        mesh=mesh,
        in_specs=(
            P(None, "expert", None),
            P("pipe", None, None),
            P("pipe", "expert", None),
            P("pipe", "expert", None),
            P("pipe", None, None, None),
            P("pipe", None, None),
        ),
        out_specs=P("pipe", None, "expert", None),
        check_vma=False,
    )
```

profile of v0, /device:TPU:0, one launch (start us, length us, event | category | flops | bytes accessed | tf_op | source)
XLA Modules:
  0.0 138.6 jit_solution(14568044816781589299)
XLA Ops:
  6.5 0.7 fusion.38
  7.3 0.2 reduce_window_sum.19
  7.5 0.2 fusion.35
  7.7 95.9 %while.21 = (s32[]{:T(128)}, bf16[32,5120]{1,0:T(8,128)(2,1)}, bf16[1,32,5120]{2,1,0:T(8,128)(2,1)}, pred[]{:T(512)}, bf16[1,32,5120]{2,1,0:T(8,128)(2,1)}, /*in...) while((s32[]{:T(128)}, bf16[32,5120]{1,0:T(8,128)(2,1)}, ...), condition=%wide.region_4.5_spmd.clone, body=%wide.region_1.4_spmd.clone.sunk | while | flops 71040296 | bytes 23656336 | solution.py:96
  7.7 5.0 %collective-permute-start = (bf16[32,5120]{1,0:T(8,128)(2,1)S(1)}, bf16[32,5120]{1,0:T(8,128)(2,1)S(1)}, u32[]{:S(2)}, u32[]{:S(2)}) collective-permute-start(bf16[32,5120]{1,0:T(8,128)(2,1)S(1)} %broadcast_select_fusion.3), channel_id=1, source_target_pairs={{0,16},{1,17},{2,18},{3,19},{4,20},{5,21},{6,22},{7,23},{8,24},{9,... | collective-permute-start | bytes 983048 | tf_op jit(solution)/shard_map/while/body/eval_jaxpr/ppermute | solution.py:12
  12.7 6.9 %collective-permute-done = bf16[32,5120]{1,0:T(8,128)(2,1)S(1)} collective-permute-done((bf16[32,5120]{1,0:T(8,128)(2,1)S(1)}, bf16[32,5120]{1,0:T(8,128)(2,1)S(1)}, u32[]{:S(2)}, u32[]{:S(2)}) %collective-permute-start) | collective-permute-done | bytes 327712 | tf_op jit(solution)/shard_map/while/body/eval_jaxpr/ppermute | solution.py:12
  19.7 1.2 fusion.64
  20.9 0.2 fusion.65
  21.2 0.6 broadcast.199
  21.8 0.8 reduce.13
  22.6 14.2 %all_to_all.32 = bf16[16,2,2560]{2,1,0:T(2,128)(2,1)S(1)} all-to-all(bf16[16,2,2560]{2,1,0:T(2,128)(2,1)S(1)} %reshape.138), channel_id=1, replica_groups=mesh['pipe'=2,'expert'=16] {'expert'}, dimensions={0} | all-to-all | bytes 327680 | tf_op jit(solution)/shard_map/while/body/eval_jaxpr/all_to_all | solution.py:66
  36.8 0.1 reshape.139
  37.0 3.0 %fusion.66 = bf16[16,1,5120]{2,0,1:T(8,128)(2,1)S(1)} fusion(bf16[1,192,5120]{2,1,0:T(8,128)(2,1)} %get-tuple-element.587, bf16[1,192,5120]{2,1,0:T(8,128)(2,1)S(1)} %copy-done.1, bf16[16,1,5120]{2,1,0:T(2,128)(2,1)S(1)} %reshape.139), kind=kOutput, calls=%fused_computation.3.clone.1 | convolution fusion | flops 63011840 | bytes 4259840 | tf_op jit(solution)/shard_map/while/body/eval_jaxpr/dot_general | solution.py:45
  40.0 0.6 broadcast.200
  40.6 0.8 reduce.14
  41.4 0.8 reshape.140
  42.1 3.5 %all-to-all-start.1 = ((bf16[16,2,2560]{2,1,0:T(2,128)(2,1)}), bf16[16,2,2560]{2,1,0:T(2,128)(2,1)S(1)}, u32[]{:S(2)}, u32[]{:S(2)}) async-start(bf16[16,2,2560]{2,1,0:T(2,128)(2,1)} %reshape.140), calls=%async_computation.1 | async-start | bytes 327680 | tf_op jit(solution)/shard_map/while/body/eval_jaxpr/all_to_all | solution.py:68
  45.7 0.3 fusion.67
  45.9 8.1 %all-to-all-done.1 = bf16[16,2,2560]{2,1,0:T(2,128)(2,1)S(1)} async-done(((bf16[16,2,2560]{2,1,0:T(2,128)(2,1)}), bf16[16,2,2560]{2,1,0:T(2,128)(2,1)S(1)}, u32[]{:S(2)}, u32[]{:S(2)}) %all-to-all-start.1) | async-done | bytes 163872 | tf_op jit(solution)/shard_map/while/body/eval_jaxpr/all_to_all | solution.py:68
  54.0 0.1 reshape.141
  54.2 0.3 reshape.142
  54.5 0.1 bitcast_reduce_fusion.2
  54.7 1.6 %bitcast_select_fusion.4 = (bf16[1,32,5120]{2,1,0:T(8,128)(2,1)S(1)}, bf16[32,5120]{1,0:T(8,128)(2,1)}) fusion(bf16[1,32,5120]{2,1,0:T(8,128)(2,1)S(1)} %copy-done.2, pred[]{:T(512)S(6)} %compare.3, pred[]{:T(512)S(6)} %and.69, f32[2,32]{1,0:T(2,128)S(1)} %fusion.67, f32[2,5120]{1,0:T(2,128)S(1)} %bitcast_reduce_fusion.2, ...), kind=kOutput, calls=%fused_computation.20.clone.1 | convolution fusion | flops 4751360 | bytes 1351938 | tf_op jit(solution)/shard_map/while/body/eval_jaxpr/ert,erd->td/dot_general | solution.py:73
  56.2 0.7 copy-done.3
  57.0 1.1 broadcast_select_fusion.3
  58.1 4.4 %collective-permute-start = (bf16[32,5120]{1,0:T(8,128)(2,1)S(1)}, bf16[32,5120]{1,0:T(8,128)(2,1)S(1)}, u32[]{:S(2)}, u32[]{:S(2)}) collective-permute-start(bf16[32,5120]{1,0:T(8,128)(2,1)S(1)} %broadcast_select_fusion.3), channel_id=1, source_target_pairs={{0,16},{1,17},{2,18},{3,19},{4,20},{5,21},{6,22},{7,23},{8,24},{9,... | collective-permute-start | bytes 983048 | tf_op jit(solution)/shard_map/while/body/eval_jaxpr/ppermute | solution.py:12
  62.5 6.3 %collective-permute-done = bf16[32,5120]{1,0:T(8,128)(2,1)S(1)} collective-permute-done((bf16[32,5120]{1,0:T(8,128)(2,1)S(1)}, bf16[32,5120]{1,0:T(8,128)(2,1)S(1)}, u32[]{:S(2)}, u32[]{:S(2)}) %collective-permute-start) | collective-permute-done | bytes 327712 | tf_op jit(solution)/shard_map/while/body/eval_jaxpr/ppermute | solution.py:12
  68.9 1.2 fusion.64
  70.1 0.2 fusion.65
  70.4 0.6 broadcast.199
  71.0 0.8 reduce.13
  71.8 11.6 %all_to_all.32 = bf16[16,2,2560]{2,1,0:T(2,128)(2,1)S(1)} all-to-all(bf16[16,2,2560]{2,1,0:T(2,128)(2,1)S(1)} %reshape.138), channel_id=1, replica_groups=mesh['pipe'=2,'expert'=16] {'expert'}, dimensions={0} | all-to-all | bytes 327680 | tf_op jit(solution)/shard_map/while/body/eval_jaxpr/all_to_all | solution.py:66
  83.6 3.0 %fusion.66 = bf16[16,1,5120]{2,0,1:T(8,128)(2,1)S(1)} fusion(bf16[1,192,5120]{2,1,0:T(8,128)(2,1)} %get-tuple-element.587, bf16[1,192,5120]{2,1,0:T(8,128)(2,1)S(1)} %copy-done.1, bf16[16,1,5120]{2,1,0:T(2,128)(2,1)S(1)} %reshape.139), kind=kOutput, calls=%fused_computation.3.clone.1 | convolution fusion | flops 63011840 | bytes 4259840 | tf_op jit(solution)/shard_map/while/body/eval_jaxpr/dot_general | solution.py:45
  86.6 0.6 broadcast.200
  87.2 0.8 reduce.14
  88.0 0.8 reshape.140
  88.7 3.5 %all-to-all-start.1 = ((bf16[16,2,2560]{2,1,0:T(2,128)(2,1)}), bf16[16,2,2560]{2,1,0:T(2,128)(2,1)S(1)}, u32[]{:S(2)}, u32[]{:S(2)}) async-start(bf16[16,2,2560]{2,1,0:T(2,128)(2,1)} %reshape.140), calls=%async_computation.1 | async-start | bytes 327680 | tf_op jit(solution)/shard_map/while/body/eval_jaxpr/all_to_all | solution.py:68
  92.3 0.3 fusion.67
  92.6 8.1 %all-to-all-done.1 = bf16[16,2,2560]{2,1,0:T(2,128)(2,1)S(1)} async-done(((bf16[16,2,2560]{2,1,0:T(2,128)(2,1)}), bf16[16,2,2560]{2,1,0:T(2,128)(2,1)S(1)}, u32[]{:S(2)}, u32[]{:S(2)}) %all-to-all-start.1) | async-done | bytes 163872 | tf_op jit(solution)/shard_map/while/body/eval_jaxpr/all_to_all | solution.py:68
  100.7 0.1 reshape.141
  100.8 0.3 reshape.142
  101.1 0.1 bitcast_reduce_fusion.2
  101.3 1.6 %bitcast_select_fusion.4 = (bf16[1,32,5120]{2,1,0:T(8,128)(2,1)S(1)}, bf16[32,5120]{1,0:T(8,128)(2,1)}) fusion(bf16[1,32,5120]{2,1,0:T(8,128)(2,1)S(1)} %copy-done.2, pred[]{:T(512)S(6)} %compare.3, pred[]{:T(512)S(6)} %and.69, f32[2,32]{1,0:T(2,128)S(1)} %fusion.67, f32[2,5120]{1,0:T(2,128)S(1)} %bitcast_reduce_fusion.2, ...), kind=kOutput, calls=%fused_computation.20.clone.1 | convolution fusion | flops 4751360 | bytes 1351938 | tf_op jit(solution)/shard_map/while/body/eval_jaxpr/ert,erd->td/dot_general | solution.py:73
  102.9 0.7 copy-done.3
  103.6 0.7 broadcast_select_fusion.1
  104.4 24.3 %all-reduce.2.cloned.1.call-done = bf16[1,32,5120]{2,1,0:T(8,128)(2,1)} async-done(((bf16[1,32,5120]{2,1,0:T(8,128)(2,1)}), bf16[1,32,5120]{2,1,0:T(8,128)(2,1)}) %all-reduce.2.cloned.1.call-update) | async-done | bytes 327696 | tf_op jit(solution)/shard_map/psum | solution.py:17
  128.6 1.1 fusion.29
  129.8 1.9 %fusion.28 = bf16[1,1,32,64]{3,2,1,0:T(8,128)(2,1)} fusion(bf16[1,64,5120]{2,1,0:T(8,128)(2,1)S(1)} %copy-done, bf16[1,32,5120]{2,1,0:T(8,128)(2,1)} %all-reduce.2.cloned.1.call-done, f32[32]{0:T(128)S(1)} %add_rsqrt_fusion.1), kind=kOutput, calls=%fused_computation.32 | convolution fusion | flops 21465088 | bytes 987264 | tf_op jit(solution)/shard_map/mtd,jd->mtj/dot_general | solution.py:99
  (31 shorter events, 0.5 us)
Async XLA Ops:
  6.5 123.3 %copy-start = (bf16[1,64,5120]{2,1,0:T(8,128)(2,1)S(1)}, bf16[1,64,5120]{2,1,0:T(8,128)(2,1)}, u32[]{:S(2)}) copy-start(bf16[1,64,5120]{2,1,0:T(8,128)(2,1)} %param.13) | copy-start | bytes 1966084
  6.5 122.1 %all-reduce.2.cloned.1.call-start = ((), (), s32[]{:S(2)}) async-start(), calls=%async_computation.2 | async-start | bytes 655360 | tf_op jit(solution)/shard_map/psum | solution.py:17
  7.7 29.3 %copy-start.1 = (bf16[1,192,5120]{2,1,0:T(8,128)(2,1)S(1)}, bf16[1,192,5120]{2,1,0:T(8,128)(2,1)}, u32[]{:S(2)}) copy-start(bf16[1,192,5120]{2,1,0:T(8,128)(2,1)} %get-tuple-element.586) | copy-start | bytes 5898244 | tf_op jit(solution)/shard_map/while
  7.7 12.0 %collective-permute-start = (bf16[32,5120]{1,0:T(8,128)(2,1)S(1)}, bf16[32,5120]{1,0:T(8,128)(2,1)S(1)}, u32[]{:S(2)}, u32[]{:S(2)}) collective-permute-start(bf16[32,5120]{1,0:T(8,128)(2,1)S(1)} %broadcast_select_fusion.3), channel_id=1, source_target_pairs={{0,16},{1,17},{2,18},{3,19},{4,20},{5,21},{6,22},{7,23},{8,24},{9,... | collective-permute-start | bytes 983048 | tf_op jit(solution)/shard_map/while/body/eval_jaxpr/ppermute | solution.py:12
  36.9 8.7 %copy-start.4 = (bf16[1,5120,2]{1,2,0:T(2,128)(2,1)S(1)}, bf16[1,5120,2]{1,2,0:T(2,128)(2,1)}, u32[]{:S(2)}) copy-start(bf16[1,5120,2]{1,2,0:T(2,128)(2,1)} %get-tuple-element.583) | copy-start | bytes 61444 | tf_op jit(solution)/shard_map/while
  40.0 14.7 %copy-start.2 = (bf16[1,32,5120]{2,1,0:T(8,128)(2,1)S(1)}, bf16[1,32,5120]{2,1,0:T(8,128)(2,1)}, u32[]{:S(2)}) copy-start(bf16[1,32,5120]{2,1,0:T(8,128)(2,1)} %get-tuple-element.564) | copy-start | bytes 983044 | tf_op jit(solution)/shard_map/while
  42.1 11.9 %all-to-all-start.1 = ((bf16[16,2,2560]{2,1,0:T(2,128)(2,1)}), bf16[16,2,2560]{2,1,0:T(2,128)(2,1)S(1)}, u32[]{:S(2)}, u32[]{:S(2)}) async-start(bf16[16,2,2560]{2,1,0:T(2,128)(2,1)} %reshape.140), calls=%async_computation.1 | async-start | bytes 327680 | tf_op jit(solution)/shard_map/while/body/eval_jaxpr/all_to_all | solution.py:68
  56.2 0.7 copy-start.3
  57.0 26.6 %copy-start.1 = (bf16[1,192,5120]{2,1,0:T(8,128)(2,1)S(1)}, bf16[1,192,5120]{2,1,0:T(8,128)(2,1)}, u32[]{:S(2)}) copy-start(bf16[1,192,5120]{2,1,0:T(8,128)(2,1)} %get-tuple-element.586) | copy-start | bytes 5898244 | tf_op jit(solution)/shard_map/while
  58.1 10.8 %collective-permute-start = (bf16[32,5120]{1,0:T(8,128)(2,1)S(1)}, bf16[32,5120]{1,0:T(8,128)(2,1)S(1)}, u32[]{:S(2)}, u32[]{:S(2)}) collective-permute-start(bf16[32,5120]{1,0:T(8,128)(2,1)S(1)} %broadcast_select_fusion.3), channel_id=1, source_target_pairs={{0,16},{1,17},{2,18},{3,19},{4,20},{5,21},{6,22},{7,23},{8,24},{9,... | collective-permute-start | bytes 983048 | tf_op jit(solution)/shard_map/while/body/eval_jaxpr/ppermute | solution.py:12
  83.6 8.7 %copy-start.4 = (bf16[1,5120,2]{1,2,0:T(2,128)(2,1)S(1)}, bf16[1,5120,2]{1,2,0:T(2,128)(2,1)}, u32[]{:S(2)}) copy-start(bf16[1,5120,2]{1,2,0:T(2,128)(2,1)} %get-tuple-element.583) | copy-start | bytes 61444 | tf_op jit(solution)/shard_map/while
  86.6 14.7 %copy-start.2 = (bf16[1,32,5120]{2,1,0:T(8,128)(2,1)S(1)}, bf16[1,32,5120]{2,1,0:T(8,128)(2,1)}, u32[]{:S(2)}) copy-start(bf16[1,32,5120]{2,1,0:T(8,128)(2,1)} %get-tuple-element.564) | copy-start | bytes 983044 | tf_op jit(solution)/shard_map/while
  88.7 11.9 %all-to-all-start.1 = ((bf16[16,2,2560]{2,1,0:T(2,128)(2,1)}), bf16[16,2,2560]{2,1,0:T(2,128)(2,1)S(1)}, u32[]{:S(2)}, u32[]{:S(2)}) async-start(bf16[16,2,2560]{2,1,0:T(2,128)(2,1)} %reshape.140), calls=%async_computation.1 | async-start | bytes 327680 | tf_op jit(solution)/shard_map/while/body/eval_jaxpr/all_to_all | solution.py:68
  102.9 0.7 copy-start.3
Sparse Core Ops, SparseCore 0:
  104.5 24.1 all-reduce.1
where the time goes:
time: 139 us
  waiting for transfers between devices  53.8 us (39%)
  blocking collectives  25.8 us (19%)
  starting transfers between devices  16.5 us (12%)
  between operations  13.4 us (10%)
  matrix products  12.4 us (9%)
  other arithmetic  10.4 us (7%)
  local copies, waits for them, and re-layouts  6.15 us (4%)
    all_to_all x2, blocking collectives, layer(): lax.all_to_all(copies, 'expert', split_axis=0, concat_axis=0, tiled=True)  25.8 us
    psum x1, waiting for transfers between devices, from_root(): return lax.psum(jnp.where(mine, x, jnp.zeros_like(x)), axis)  24.3 us
    all_to_all x2, waiting for transfers between devices, layer(): lax.all_to_all(partials, 'expert', split_axis=0, concat_axis=0, tiled=True)  16.2 us
    ppermute x2, waiting for transfers between devices, passed_along(): return lax.ppermute(x, axis, pairs)  13.3 us
    ppermute x2, starting transfers between devices, passed_along(): return lax.ppermute(x, axis, pairs)  9.43 us
    all_to_all x2, starting transfers between devices, layer(): lax.all_to_all(partials, 'expert', split_axis=0, concat_axis=0, tiled=True)  7.03 us
    dot_general x2, matrix products, expert_rows(): jnp.dot(hidden, w_down[0], preferred_element_type=jnp.float32)  6.05 us
    while x24, local copies, waits for them, and re-layouts  3.7 us
  transfers between devices with their start and end apart: 5, of which 5 were waited for; matrix products, arithmetic and copies ran while one was open for 0% of the time, Pallas kernels for 0%

commit v1 on v0

--- a/solution.py
+++ b/solution.py
@@ -4,6 +4,30 @@
 from jax.sharding import PartitionSpec as P
 
 SLOT = 1
+
+
+def cut_along(x, dim, count):
+    shape = x.shape
+    blocks = x.reshape(*shape[:dim], count, shape[dim] // count, *shape[dim + 1 :])
+    return jnp.moveaxis(blocks, dim, 0)
+
+
+def laid_out(blocks, dim):
+    blocks = jnp.moveaxis(blocks, 0, dim)
+    shape = blocks.shape
+    return blocks.reshape(*shape[:dim], shape[dim] * shape[dim + 1], *shape[dim + 2 :])
+
+
+def sent_to_each(array, axis, split_dim, concat_dim):
+    size, index = (lax.axis_size(axis), lax.axis_index(axis))
+    parts = cut_along(array, split_dim, size)
+    result = parts
+    for step in range(1, size):
+        target, source = ((index + step) % size, (index - step) % size)
+        sent = lax.dynamic_index_in_dim(parts, target, 0)
+        theirs = lax.ppermute(sent, axis, [(i, (i + step) % size) for i in range(size)])
+        result = lax.dynamic_update_slice_in_dim(result, theirs, source, axis=0)
+    return laid_out(result, concat_dim)
 
 
 def passed_along(x, axis, by):
@@ -62,9 +86,7 @@
             "ert,td->erd", selector.astype(jnp.bfloat16), normed, preferred_element_type=jnp.float32
         ).astype(jnp.bfloat16)
         copies = jnp.repeat(picked, group_size, axis=0)
-        partials = expert_rows(
-            lax.all_to_all(copies, "expert", split_axis=0, concat_axis=0, tiled=True)
-        )
+        partials = expert_rows(sent_to_each(copies, "expert", 0, 0))
         returned = lax.all_to_all(partials, "expert", split_axis=0, concat_axis=0, tiled=True)
         expert_out = jnp.sum(
             returned.astype(jnp.float32).reshape(experts, group_size, SLOT, features), axis=1

time: 139 us -> 160 us (1.15)
  starting transfers between devices: 16.5 us -> 57.4 us
  blocking collectives: 25.8 us -> 0 us
  local copies, waits for them, and re-layouts: 6.15 us -> 13.5 us
  other arithmetic: 10.4 us -> 7.52 us
  waiting for transfers between devices: 53.8 us -> 56 us
    ppermute x0 -> x30, starting transfers between devices: none -> 41.1 us  [sent_to_each(): lax.ppermute(sent, axis, [(i, (i + step) % size) for i in range(size)])]
    all_to_all x2 -> x0, blocking collectives: 25.8 us -> none  [layer(): lax.all_to_all(copies, 'expert', split_axis=0, concat_axis=0, tiled=True)]
    dynamic_update_slice x0 -> x30, local copies, waits for them, and re-layouts: none -> 8.48 us  [sent_to_each(): result = lax.dynamic_update_slice_in_dim(result, theirs, source, axis=0)]
    ppermute x0 -> x30, waiting for transfers between devices: none -> 2.67 us  [sent_to_each(): lax.ppermute(sent, axis, [(i, (i + step) % size) for i in range(size)])]
    while x24 -> x20, local copies, waits for them, and re-layouts: 3.7 us -> 3.23 us
  transfers between devices with their start and end apart: 5 -> 35, of which waited for: 5 -> 7; matrix products, arithmetic and copies ran while one was open for 0% -> 5% of each run, Pallas kernels for 0% -> 0%
where the time goes in v1:
time: 160 us
  starting transfers between devices  57.4 us (36%)
  waiting for transfers between devices  56 us (35%)
  local copies, waits for them, and re-layouts  13.5 us (8%)
  between operations  13.4 us (8%)
  matrix products  11 us (7%)
  other arithmetic  7.52 us (5%)
    ppermute x30, starting transfers between devices, sent_to_each(): lax.ppermute(sent, axis, [(i, (i + step) % size) for i in range(size)])  41.1 us
    psum x1, waiting for transfers between devices, from_root(): return lax.psum(jnp.where(mine, x, jnp.zeros_like(x)), axis)  24.3 us
    all_to_all x2, waiting for transfers between devices, layer(): lax.all_to_all(partials, 'expert', split_axis=0, concat_axis=0, tiled=True)  16.2 us
    ppermute x2, waiting for transfers between devices, passed_along(): return lax.ppermute(x, axis, pairs)  12.8 us
    ppermute x2, starting transfers between devices, passed_along(): return lax.ppermute(x, axis, pairs)  9.29 us
    dynamic_update_slice x30, local copies, waits for them, and re-layouts, sent_to_each(): result = lax.dynamic_update_slice_in_dim(result, theirs, source, axis=0)  8.48 us
    all_to_all x2, starting transfers between devices, layer(): lax.all_to_all(partials, 'expert', split_axis=0, concat_axis=0, tiled=True)  7.03 us
    dot_general x2, matrix products, expert_rows(): jnp.dot(hidden, w_down[0], preferred_element_type=jnp.float32)  6.05 us
  transfers between devices with their start and end apart: 35, of which 7 were waited for; matrix products, arithmetic and copies ran while one was open for 5% of the time, Pallas kernels for 0%

profile of v1, /device:TPU:0, one launch (start us, length us, event | category | flops | bytes accessed | tf_op | source)
XLA Modules:
  0.0 159.9 jit_solution(3570342257433782002)
XLA Ops:
  6.5 0.7 fusion.32
  7.7 117.2 %while.21 = (s32[]{:T(128)}, bf16[32,5120]{1,0:T(8,128)(2,1)S(1)}, bf16[1,32,5120]{2,1,0:T(8,128)(2,1)}, pred[]{:T(512)}, bf16[1,32,5120]{2,1,0:T(8,128)(2,1)}, ...) while((s32[]{:T(128)}, bf16[32,5120]{1,0:T(8,128)(2,1)S(1)}, ...), condition=%wide.region_4.5_spmd.clone, body=%wide.region_1.4_spmd.clone.sunk | while | flops 71040752 | bytes 23743880 | solution.py:118
  7.7 4.9 %collective-permute-start = (bf16[32,5120]{1,0:T(8,128)(2,1)S(1)}, bf16[32,5120]{1,0:T(8,128)(2,1)S(1)}, u32[]{:S(2)}, u32[]{:S(2)}) collective-permute-start(bf16[32,5120]{1,0:T(8,128)(2,1)S(1)} %broadcast_select_fusion.3), channel_id=1, source_target_pairs={{0,16},{1,17},{2,18},{3,19},{4,20},{5,21},{6,22},{7,23},{8,24},{9,... | collective-permute-start | bytes 983048 | tf_op jit(solution)/shard_map/while/body/eval_jaxpr/ppermute | solution.py:36
  12.8 6.7 %collective-permute-done = bf16[32,5120]{1,0:T(8,128)(2,1)S(1)} collective-permute-done((bf16[32,5120]{1,0:T(8,128)(2,1)S(1)}, bf16[32,5120]{1,0:T(8,128)(2,1)S(1)}, u32[]{:S(2)}, u32[]{:S(2)}) %collective-permute-start) | collective-permute-done | bytes 327712 | tf_op jit(solution)/shard_map/while/body/eval_jaxpr/ppermute | solution.py:36
  19.5 1.2 fusion.59
  21.5 1.6 collective-permute-start.2
  23.1 2.4 %collective-permute-start.3 = (bf16[1,1,1,5120]{3,0,2,1:T(2,128)(2,1)S(1)}, bf16[1,1,1,5120]{3,0,2,1:T(2,128)(2,1)S(1)}, u32[]{:S(2)}, u32[]{:S(2)}) collective-permute-start(bf16[1,1,1,5120]{3,0,2,1:T(2,128)(2,1)S(1)} %get-tuple-element.610), channel_id=1, source_target_pairs={{0,3},{1,4},{2,5},{3,6},{4,7},{5,8},{6,9},{7,10},{8,11},{9,12},{10... | collective-permute-start | bytes 30728 | tf_op jit(solution)/shard_map/while/body/eval_jaxpr/ppermute | solution.py:28
  25.5 1.6 collective-permute-start.4
  27.4 1.0 collective-permute-start.6
  28.4 4.3 %collective-permute-start.7 = (bf16[1,1,1,5120]{3,0,2,1:T(2,128)(2,1)S(1)}, bf16[1,1,1,5120]{3,0,2,1:T(2,128)(2,1)S(1)}, u32[]{:S(2)}, u32[]{:S(2)}) collective-permute-start(bf16[1,1,1,5120]{3,0,2,1:T(2,128)(2,1)S(1)} %get-tuple-element.614), channel_id=1, source_target_pairs={{0,7},{1,8},{2,9},{3,10},{4,11},{5,12},{6,13},{7,14},{8,15},{9,0},... | collective-permute-start | bytes 30728 | tf_op jit(solution)/shard_map/while/body/eval_jaxpr/ppermute | solution.py:28
  33.4 2.4 %collective-permute-start.10 = (bf16[1,1,1,5120]{3,0,2,1:T(2,128)(2,1)S(1)}, bf16[1,1,1,5120]{3,0,2,1:T(2,128)(2,1)S(1)}, u32[]{:S(2)}, u32[]{:S(2)}) collective-permute-start(bf16[1,1,1,5120]{3,0,2,1:T(2,128)(2,1)S(1)} %get-tuple-element.617), channel_id=1, source_target_pairs={{0,10},{1,11},{2,12},{3,13},{4,14},{5,15},{6,0},{7,1},{8,2},{9,3},... | collective-permute-start | bytes 30728 | tf_op jit(solution)/shard_map/while/body/eval_jaxpr/ppermute | solution.py:28
  35.8 2.9 %collective-permute-start.11 = (bf16[1,1,1,5120]{3,0,2,1:T(2,128)(2,1)S(1)}, bf16[1,1,1,5120]{3,0,2,1:T(2,128)(2,1)S(1)}, u32[]{:S(2)}, u32[]{:S(2)}) collective-permute-start(bf16[1,1,1,5120]{3,0,2,1:T(2,128)(2,1)S(1)} %get-tuple-element.618), channel_id=1, source_target_pairs={{0,11},{1,12},{2,13},{3,14},{4,15},{5,0},{6,1},{7,2},{8,3},{9,4},{... | collective-permute-start | bytes 30728 | tf_op jit(solution)/shard_map/while/body/eval_jaxpr/ppermute | solution.py:28
  38.7 1.8 %collective-permute-start.12 = (bf16[1,1,1,5120]{3,0,2,1:T(2,128)(2,1)S(1)}, bf16[1,1,1,5120]{3,0,2,1:T(2,128)(2,1)S(1)}, u32[]{:S(2)}, u32[]{:S(2)}) collective-permute-start(bf16[1,1,1,5120]{3,0,2,1:T(2,128)(2,1)S(1)} %get-tuple-element.619), channel_id=1, source_target_pairs={{0,12},{1,13},{2,14},{3,15},{4,0},{5,1},{6,2},{7,3},{8,4},{9,5},{1... | collective-permute-start | bytes 30728 | tf_op jit(solution)/shard_map/while/body/eval_jaxpr/ppermute | solution.py:28
  40.5 1.5 collective-permute-start.14
  42.0 2.2 %collective-permute-start.15 = (bf16[1,1,1,5120]{3,0,2,1:T(2,128)(2,1)S(1)}, bf16[1,1,1,5120]{3,0,2,1:T(2,128)(2,1)S(1)}, u32[]{:S(2)}, u32[]{:S(2)}) collective-permute-start(bf16[1,1,1,5120]{3,0,2,1:T(2,128)(2,1)S(1)} %get-tuple-element.622), channel_id=1, source_target_pairs={{0,15},{1,0},{2,1},{3,2},{4,3},{5,4},{6,5},{7,6},{8,7},{9,8},{10,9... | collective-permute-start | bytes 30728 | tf_op jit(solution)/shard_map/while/body/eval_jaxpr/ppermute | solution.py:28
  48.6 3.0 %fusion.61 = bf16[16,1,5120]{2,0,1:T(8,128)(2,1)S(1)} fusion(bf16[1,192,5120]{2,1,0:T(8,128)(2,1)} %get-tuple-element.726, bf16[16,5120]{1,0:T(8,128)(2,1)S(1)} %dynamic_update_slice.258, bf16[1,192,5120]{2,1,0:T(8,128)(2,1)S(1)} %copy-done.1), kind=kOutput, calls=%fused_computation.3.clone.1 | convolution fusion | flops 63011840 | bytes 4259840 | tf_op jit(solution)/shard_map/while/body/eval_jaxpr/dot_general | solution.py:69
  52.1 0.6 reduce.12
  52.7 0.8 reshape.335
  53.5 3.5 %all-to-all-start = ((bf16[16,2,2560]{2,1,0:T(2,128)(2,1)}), bf16[16,2,2560]{2,1,0:T(2,128)(2,1)S(1)}, u32[]{:S(2)}, u32[]{:S(2)}) async-start(bf16[16,2,2560]{2,1,0:T(2,128)(2,1)} %reshape.335), calls=%async_computation | async-start | bytes 327680 | tf_op jit(solution)/shard_map/while/body/eval_jaxpr/all_to_all | solution.py:90
  57.3 8.1 %all-to-all-done = bf16[16,2,2560]{2,1,0:T(2,128)(2,1)S(1)} async-done(((bf16[16,2,2560]{2,1,0:T(2,128)(2,1)}), bf16[16,2,2560]{2,1,0:T(2,128)(2,1)S(1)}, u32[]{:S(2)}, u32[]{:S(2)}) %all-to-all-start) | async-done | bytes 163872 | tf_op jit(solution)/shard_map/while/body/eval_jaxpr/all_to_all | solution.py:90
  66.0 0.9 bitcast_select_fusion.4
  66.9 0.7 copy-done.3
  67.7 4.4 %collective-permute-start = (bf16[32,5120]{1,0:T(8,128)(2,1)S(1)}, bf16[32,5120]{1,0:T(8,128)(2,1)S(1)}, u32[]{:S(2)}, u32[]{:S(2)}) collective-permute-start(bf16[32,5120]{1,0:T(8,128)(2,1)S(1)} %broadcast_select_fusion.3), channel_id=1, source_target_pairs={{0,16},{1,17},{2,18},{3,19},{4,20},{5,21},{6,22},{7,23},{8,24},{9,... | collective-permute-start | bytes 983048 | tf_op jit(solution)/shard_map/while/body/eval_jaxpr/ppermute | solution.py:36
  72.3 6.1 %collective-permute-done = bf16[32,5120]{1,0:T(8,128)(2,1)S(1)} collective-permute-done((bf16[32,5120]{1,0:T(8,128)(2,1)S(1)}, bf16[32,5120]{1,0:T(8,128)(2,1)S(1)}, u32[]{:S(2)}, u32[]{:S(2)}) %collective-permute-start) | collective-permute-done | bytes 327712 | tf_op jit(solution)/shard_map/while/body/eval_jaxpr/ppermute | solution.py:36
  78.4 1.2 fusion.59
  80.4 0.7 collective-permute-start.2
  81.1 1.8 %collective-permute-start.3 = (bf16[1,1,1,5120]{3,0,2,1:T(2,128)(2,1)S(1)}, bf16[1,1,1,5120]{3,0,2,1:T(2,128)(2,1)S(1)}, u32[]{:S(2)}, u32[]{:S(2)}) collective-permute-start(bf16[1,1,1,5120]{3,0,2,1:T(2,128)(2,1)S(1)} %get-tuple-element.610), channel_id=1, source_target_pairs={{0,3},{1,4},{2,5},{3,6},{4,7},{5,8},{6,9},{7,10},{8,11},{9,12},{10... | collective-permute-start | bytes 30728 | tf_op jit(solution)/shard_map/while/body/eval_jaxpr/ppermute | solution.py:28
  82.9 0.6 collective-permute-start.4
  83.8 2.5 %collective-permute-done.1 = bf16[1,1,1,5120]{3,0,2,1:T(2,128)(2,1)S(1)} collective-permute-done((bf16[1,1,1,5120]{3,0,2,1:T(2,128)(2,1)S(1)}, bf16[1,1,1,5120]{3,0,2,1:T(2,128)(2,1)S(1)}, u32[]{:S(2)}, u32[]{:S(2)}) %collective-permute-start.1) | collective-permute-done | bytes 10272 | tf_op jit(solution)/shard_map/while/body/eval_jaxpr/ppermute | solution.py:28
  86.3 0.9 collective-permute-start.6
  87.1 2.6 %collective-permute-start.7 = (bf16[1,1,1,5120]{3,0,2,1:T(2,128)(2,1)S(1)}, bf16[1,1,1,5120]{3,0,2,1:T(2,128)(2,1)S(1)}, u32[]{:S(2)}, u32[]{:S(2)}) collective-permute-start(bf16[1,1,1,5120]{3,0,2,1:T(2,128)(2,1)S(1)} %get-tuple-element.614), channel_id=1, source_target_pairs={{0,7},{1,8},{2,9},{3,10},{4,11},{5,12},{6,13},{7,14},{8,15},{9,0},... | collective-permute-start | bytes 30728 | tf_op jit(solution)/shard_map/while/body/eval_jaxpr/ppermute | solution.py:28
  89.7 1.5 collective-permute-start.8
  91.3 1.8 %collective-permute-start.10 = (bf16[1,1,1,5120]{3,0,2,1:T(2,128)(2,1)S(1)}, bf16[1,1,1,5120]{3,0,2,1:T(2,128)(2,1)S(1)}, u32[]{:S(2)}, u32[]{:S(2)}) collective-permute-start(bf16[1,1,1,5120]{3,0,2,1:T(2,128)(2,1)S(1)} %get-tuple-element.617), channel_id=1, source_target_pairs={{0,10},{1,11},{2,12},{3,13},{4,14},{5,15},{6,0},{7,1},{8,2},{9,3},... | collective-permute-start | bytes 30728 | tf_op jit(solution)/shard_map/while/body/eval_jaxpr/ppermute | solution.py:28
  93.1 3.6 %collective-permute-start.11 = (bf16[1,1,1,5120]{3,0,2,1:T(2,128)(2,1)S(1)}, bf16[1,1,1,5120]{3,0,2,1:T(2,128)(2,1)S(1)}, u32[]{:S(2)}, u32[]{:S(2)}) collective-permute-start(bf16[1,1,1,5120]{3,0,2,1:T(2,128)(2,1)S(1)} %get-tuple-element.618), channel_id=1, source_target_pairs={{0,11},{1,12},{2,13},{3,14},{4,15},{5,0},{6,1},{7,2},{8,3},{9,4},{... | collective-permute-start | bytes 30728 | tf_op jit(solution)/shard_map/while/body/eval_jaxpr/ppermute | solution.py:28
  96.8 1.0 collective-permute-start.13
  97.9 1.5 collective-permute-start.14
  99.4 2.0 %collective-permute-start.15 = (bf16[1,1,1,5120]{3,0,2,1:T(2,128)(2,1)S(1)}, bf16[1,1,1,5120]{3,0,2,1:T(2,128)(2,1)S(1)}, u32[]{:S(2)}, u32[]{:S(2)}) collective-permute-start(bf16[1,1,1,5120]{3,0,2,1:T(2,128)(2,1)S(1)} %get-tuple-element.622), channel_id=1, source_target_pairs={{0,15},{1,0},{2,1},{3,2},{4,3},{5,4},{6,5},{7,6},{8,7},{9,8},{10,9... | collective-permute-start | bytes 30728 | tf_op jit(solution)/shard_map/while/body/eval_jaxpr/ppermute | solution.py:28
  105.8 3.0 %fusion.61 = bf16[16,1,5120]{2,0,1:T(8,128)(2,1)S(1)} fusion(bf16[1,192,5120]{2,1,0:T(8,128)(2,1)} %get-tuple-element.726, bf16[16,5120]{1,0:T(8,128)(2,1)S(1)} %dynamic_update_slice.258, bf16[1,192,5120]{2,1,0:T(8,128)(2,1)S(1)} %copy-done.1), kind=kOutput, calls=%fused_computation.3.clone.1 | convolution fusion | flops 63011840 | bytes 4259840 | tf_op jit(solution)/shard_map/while/body/eval_jaxpr/dot_general | solution.py:69
  109.4 0.6 reduce.12
  110.0 0.8 reshape.335
  110.7 3.5 %all-to-all-start = ((bf16[16,2,2560]{2,1,0:T(2,128)(2,1)}), bf16[16,2,2560]{2,1,0:T(2,128)(2,1)S(1)}, u32[]{:S(2)}, u32[]{:S(2)}) async-start(bf16[16,2,2560]{2,1,0:T(2,128)(2,1)} %reshape.335), calls=%async_computation | async-start | bytes 327680 | tf_op jit(solution)/shard_map/while/body/eval_jaxpr/all_to_all | solution.py:90
  114.6 8.1 %all-to-all-done = bf16[16,2,2560]{2,1,0:T(2,128)(2,1)S(1)} async-done(((bf16[16,2,2560]{2,1,0:T(2,128)(2,1)}), bf16[16,2,2560]{2,1,0:T(2,128)(2,1)S(1)}, u32[]{:S(2)}, u32[]{:S(2)}) %all-to-all-start) | async-done | bytes 163872 | tf_op jit(solution)/shard_map/while/body/eval_jaxpr/all_to_all | solution.py:90
  123.3 0.9 bitcast_select_fusion.4
  124.2 0.7 copy-done.3
  124.9 0.8 broadcast_select_fusion.1
  125.7 24.3 %all-reduce.2.cloned.1.call-done = bf16[1,32,5120]{2,1,0:T(8,128)(2,1)} async-done(((bf16[1,32,5120]{2,1,0:T(8,128)(2,1)}), bf16[1,32,5120]{2,1,0:T(8,128)(2,1)}) %all-reduce.2.cloned.1.call-update) | async-done | bytes 327696 | tf_op jit(solution)/shard_map/psum | solution.py:41
  149.9 1.1 fusion.23
  151.1 1.9 %fusion.22 = bf16[1,1,32,64]{3,2,1,0:T(8,128)(2,1)} fusion(bf16[1,64,5120]{2,1,0:T(8,128)(2,1)S(1)} %copy-done, bf16[1,32,5120]{2,1,0:T(8,128)(2,1)} %all-reduce.2.cloned.1.call-done, f32[32]{0:T(128)S(1)} %add_rsqrt_fusion.1), kind=kOutput, calls=%fused_computation.46 | convolution fusion | flops 21465088 | bytes 987264 | tf_op jit(solution)/shard_map/mtd,jd->mtj/dot_general | solution.py:121
  (113 shorter events, 14.6 us)
Async XLA Ops:
  6.5 144.6 %copy-start = (bf16[1,64,5120]{2,1,0:T(8,128)(2,1)S(1)}, bf16[1,64,5120]{2,1,0:T(8,128)(2,1)}, u32[]{:S(2)}) copy-start(bf16[1,64,5120]{2,1,0:T(8,128)(2,1)} %param.13) | copy-start | bytes 1966084
  6.5 143.4 %all-reduce.2.cloned.1.call-start = ((), (), s32[]{:S(2)}) async-start(), calls=%async_computation.1 | async-start | bytes 655360 | tf_op jit(solution)/shard_map/psum | solution.py:41
  7.7 11.8 %collective-permute-start = (bf16[32,5120]{1,0:T(8,128)(2,1)S(1)}, bf16[32,5120]{1,0:T(8,128)(2,1)S(1)}, u32[]{:S(2)}, u32[]{:S(2)}) collective-permute-start(bf16[32,5120]{1,0:T(8,128)(2,1)S(1)} %broadcast_select_fusion.3), channel_id=1, source_target_pairs={{0,16},{1,17},{2,18},{3,19},{4,20},{5,21},{6,22},{7,23},{8,24},{9,... | collective-permute-start | bytes 983048 | tf_op jit(solution)/shard_map/while/body/eval_jaxpr/ppermute | solution.py:36
  12.6 35.9 %copy-start.1 = (bf16[1,192,5120]{2,1,0:T(8,128)(2,1)S(1)}, bf16[1,192,5120]{2,1,0:T(8,128)(2,1)}, u32[]{:S(2)}) copy-start(bf16[1,192,5120]{2,1,0:T(8,128)(2,1)} %get-tuple-element.725) | copy-start | bytes 5898244 | tf_op jit(solution)/shard_map/while
  21.4 6.0 %collective-permute-start.1 = (bf16[1,1,1,5120]{3,0,2,1:T(2,128)(2,1)S(1)}, bf16[1,1,1,5120]{3,0,2,1:T(2,128)(2,1)S(1)}, u32[]{:S(2)}, u32[]{:S(2)}) collective-permute-start(bf16[1,1,1,5120]{3,0,2,1:T(2,128)(2,1)S(1)} %get-tuple-element.608), channel_id=1, source_target_pairs={{0,1},{1,2},{2,3},{3,4},{4,5},{5,6},{6,7},{7,8},{8,9},{9,10},{10,1... | collective-permute-start | bytes 30728 | tf_op jit(solution)/shard_map/while/body/eval_jaxpr/ppermute | solution.py:28
  21.5 6.9 %collective-permute-start.2 = (bf16[1,1,1,5120]{3,0,2,1:T(2,128)(2,1)S(1)}, bf16[1,1,1,5120]{3,0,2,1:T(2,128)(2,1)S(1)}, u32[]{:S(2)}, u32[]{:S(2)}) collective-permute-start(bf16[1,1,1,5120]{3,0,2,1:T(2,128)(2,1)S(1)} %get-tuple-element.609), channel_id=1, source_target_pairs={{0,2},{1,3},{2,4},{3,5},{4,6},{5,7},{6,8},{7,9},{8,10},{9,11},{10,... | collective-permute-start | bytes 30728 | tf_op jit(solution)/shard_map/while/body/eval_jaxpr/ppermute | solution.py:28
  23.1 9.7 %collective-permute-start.3 = (bf16[1,1,1,5120]{3,0,2,1:T(2,128)(2,1)S(1)}, bf16[1,1,1,5120]{3,0,2,1:T(2,128)(2,1)S(1)}, u32[]{:S(2)}, u32[]{:S(2)}) collective-permute-start(bf16[1,1,1,5120]{3,0,2,1:T(2,128)(2,1)S(1)} %get-tuple-element.610), channel_id=1, source_target_pairs={{0,3},{1,4},{2,5},{3,6},{4,7},{5,8},{6,9},{7,10},{8,11},{9,12},{10... | collective-permute-start | bytes 30728 | tf_op jit(solution)/shard_map/while/body/eval_jaxpr/ppermute | solution.py:28
  25.5 7.6 %collective-permute-start.4 = (bf16[1,1,1,5120]{3,0,2,1:T(2,128)(2,1)S(1)}, bf16[1,1,1,5120]{3,0,2,1:T(2,128)(2,1)S(1)}, u32[]{:S(2)}, u32[]{:S(2)}) collective-permute-start(bf16[1,1,1,5120]{3,0,2,1:T(2,128)(2,1)S(1)} %get-tuple-element.611), channel_id=1, source_target_pairs={{0,4},{1,5},{2,6},{3,7},{4,8},{5,9},{6,10},{7,11},{8,12},{9,13},{1... | collective-permute-start | bytes 30728 | tf_op jit(solution)/shard_map/while/body/eval_jaxpr/ppermute | solution.py:28
  27.1 6.3 %collective-permute-start.5 = (bf16[1,1,1,5120]{3,0,2,1:T(2,128)(2,1)S(1)}, bf16[1,1,1,5120]{3,0,2,1:T(2,128)(2,1)S(1)}, u32[]{:S(2)}, u32[]{:S(2)}) collective-permute-start(bf16[1,1,1,5120]{3,0,2,1:T(2,128)(2,1)S(1)} %get-tuple-element.612), channel_id=1, source_target_pairs={{0,5},{1,6},{2,7},{3,8},{4,9},{5,10},{6,11},{7,12},{8,13},{9,14},{... | collective-permute-start | bytes 30728 | tf_op jit(solution)/shard_map/while/body/eval_jaxpr/ppermute | solution.py:28
  27.4 8.4 %collective-permute-start.6 = (bf16[1,1,1,5120]{3,0,2,1:T(2,128)(2,1)S(1)}, bf16[1,1,1,5120]{3,0,2,1:T(2,128)(2,1)S(1)}, u32[]{:S(2)}, u32[]{:S(2)}) collective-permute-start(bf16[1,1,1,5120]{3,0,2,1:T(2,128)(2,1)S(1)} %get-tuple-element.613), channel_id=1, source_target_pairs={{0,6},{1,7},{2,8},{3,9},{4,10},{5,11},{6,12},{7,13},{8,14},{9,15},... | collective-permute-start | bytes 30728 | tf_op jit(solution)/shard_map/while/body/eval_jaxpr/ppermute | solution.py:28
  28.4 10.2 %collective-permute-start.7 = (bf16[1,1,1,5120]{3,0,2,1:T(2,128)(2,1)S(1)}, bf16[1,1,1,5120]{3,0,2,1:T(2,128)(2,1)S(1)}, u32[]{:S(2)}, u32[]{:S(2)}) collective-permute-start(bf16[1,1,1,5120]{3,0,2,1:T(2,128)(2,1)S(1)} %get-tuple-element.614), channel_id=1, source_target_pairs={{0,7},{1,8},{2,9},{3,10},{4,11},{5,12},{6,13},{7,14},{8,15},{9,0},... | collective-permute-start | bytes 30728 | tf_op jit(solution)/shard_map/while/body/eval_jaxpr/ppermute | solution.py:28
  32.8 7.7 %collective-permute-start.8 = (bf16[1,1,1,5120]{3,0,2,1:T(2,128)(2,1)S(1)}, bf16[1,1,1,5120]{3,0,2,1:T(2,128)(2,1)S(1)}, u32[]{:S(2)}, u32[]{:S(2)}) collective-permute-start(bf16[1,1,1,5120]{3,0,2,1:T(2,128)(2,1)S(1)} %get-tuple-element.615), channel_id=1, source_target_pairs={{0,8},{1,9},{2,10},{3,11},{4,12},{5,13},{6,14},{7,15},{8,0},{9,1},... | collective-permute-start | bytes 30728 | tf_op jit(solution)/shard_map/while/body/eval_jaxpr/ppermute | solution.py:28
  33.1 7.4 %collective-permute-start.9 = (bf16[1,1,1,5120]{3,0,2,1:T(2,128)(2,1)S(1)}, bf16[1,1,1,5120]{3,0,2,1:T(2,128)(2,1)S(1)}, u32[]{:S(2)}, u32[]{:S(2)}) collective-permute-start(bf16[1,1,1,5120]{3,0,2,1:T(2,128)(2,1)S(1)} %get-tuple-element.616), channel_id=1, source_target_pairs={{0,9},{1,10},{2,11},{3,12},{4,13},{5,14},{6,15},{7,0},{8,1},{9,2},... | collective-permute-start | bytes 30728 | tf_op jit(solution)/shard_map/while/body/eval_jaxpr/ppermute | solution.py:28
  33.4 8.6 %collective-permute-start.10 = (bf16[1,1,1,5120]{3,0,2,1:T(2,128)(2,1)S(1)}, bf16[1,1,1,5120]{3,0,2,1:T(2,128)(2,1)S(1)}, u32[]{:S(2)}, u32[]{:S(2)}) collective-permute-start(bf16[1,1,1,5120]{3,0,2,1:T(2,128)(2,1)S(1)} %get-tuple-element.617), channel_id=1, source_target_pairs={{0,10},{1,11},{2,12},{3,13},{4,14},{5,15},{6,0},{7,1},{8,2},{9,3},... | collective-permute-start | bytes 30728 | tf_op jit(solution)/shard_map/while/body/eval_jaxpr/ppermute | solution.py:28
  35.8 11.2 %collective-permute-start.11 = (bf16[1,1,1,5120]{3,0,2,1:T(2,128)(2,1)S(1)}, bf16[1,1,1,5120]{3,0,2,1:T(2,128)(2,1)S(1)}, u32[]{:S(2)}, u32[]{:S(2)}) collective-permute-start(bf16[1,1,1,5120]{3,0,2,1:T(2,128)(2,1)S(1)} %get-tuple-element.618), channel_id=1, source_target_pairs={{0,11},{1,12},{2,13},{3,14},{4,15},{5,0},{6,1},{7,2},{8,3},{9,4},{... | collective-permute-start | bytes 30728 | tf_op jit(solution)/shard_map/while/body/eval_jaxpr/ppermute | solution.py:28
  38.7 8.7 %collective-permute-start.12 = (bf16[1,1,1,5120]{3,0,2,1:T(2,128)(2,1)S(1)}, bf16[1,1,1,5120]{3,0,2,1:T(2,128)(2,1)S(1)}, u32[]{:S(2)}, u32[]{:S(2)}) collective-permute-start(bf16[1,1,1,5120]{3,0,2,1:T(2,128)(2,1)S(1)} %get-tuple-element.619), channel_id=1, source_target_pairs={{0,12},{1,13},{2,14},{3,15},{4,0},{5,1},{6,2},{7,3},{8,4},{9,5},{1... | collective-permute-start | bytes 30728 | tf_op jit(solution)/shard_map/while/body/eval_jaxpr/ppermute | solution.py:28
  40.5 7.2 %collective-permute-start.13 = (bf16[1,1,1,5120]{3,0,2,1:T(2,128)(2,1)S(1)}, bf16[1,1,1,5120]{3,0,2,1:T(2,128)(2,1)S(1)}, u32[]{:S(2)}, u32[]{:S(2)}) collective-permute-start(bf16[1,1,1,5120]{3,0,2,1:T(2,128)(2,1)S(1)} %get-tuple-element.620), channel_id=1, source_target_pairs={{0,13},{1,14},{2,15},{3,0},{4,1},{5,2},{6,3},{7,4},{8,5},{9,6},{10... | collective-permute-start | bytes 30728 | tf_op jit(solution)/shard_map/while/body/eval_jaxpr/ppermute | solution.py:28
  40.5 7.5 %collective-permute-start.14 = (bf16[1,1,1,5120]{3,0,2,1:T(2,128)(2,1)S(1)}, bf16[1,1,1,5120]{3,0,2,1:T(2,128)(2,1)S(1)}, u32[]{:S(2)}, u32[]{:S(2)}) collective-permute-start(bf16[1,1,1,5120]{3,0,2,1:T(2,128)(2,1)S(1)} %get-tuple-element.621), channel_id=1, source_target_pairs={{0,14},{1,15},{2,0},{3,1},{4,2},{5,3},{6,4},{7,5},{8,6},{9,7},{10,... | collective-permute-start | bytes 30728 | tf_op jit(solution)/shard_map/while/body/eval_jaxpr/ppermute | solution.py:28
  42.0 6.3 %collective-permute-start.15 = (bf16[1,1,1,5120]{3,0,2,1:T(2,128)(2,1)S(1)}, bf16[1,1,1,5120]{3,0,2,1:T(2,128)(2,1)S(1)}, u32[]{:S(2)}, u32[]{:S(2)}) collective-permute-start(bf16[1,1,1,5120]{3,0,2,1:T(2,128)(2,1)S(1)} %get-tuple-element.622), channel_id=1, source_target_pairs={{0,15},{1,0},{2,1},{3,2},{4,3},{5,4},{6,5},{7,6},{8,7},{9,8},{10,9... | collective-permute-start | bytes 30728 | tf_op jit(solution)/shard_map/while/body/eval_jaxpr/ppermute | solution.py:28
  48.6 8.5 %copy-start.4 = (bf16[1,5120,2]{1,2,0:T(2,128)(2,1)S(1)}, bf16[1,5120,2]{1,2,0:T(2,128)(2,1)}, u32[]{:S(2)}) copy-start(bf16[1,5120,2]{1,2,0:T(2,128)(2,1)} %get-tuple-element.722) | copy-start | bytes 61444 | tf_op jit(solution)/shard_map/while
  51.6 14.4 %copy-start.2 = (bf16[1,32,5120]{2,1,0:T(8,128)(2,1)S(1)}, bf16[1,32,5120]{2,1,0:T(8,128)(2,1)}, u32[]{:S(2)}) copy-start(bf16[1,32,5120]{2,1,0:T(8,128)(2,1)} %get-tuple-element.673) | copy-start | bytes 983044 | tf_op jit(solution)/shard_map/while
  53.5 11.9 %all-to-all-start = ((bf16[16,2,2560]{2,1,0:T(2,128)(2,1)}), bf16[16,2,2560]{2,1,0:T(2,128)(2,1)S(1)}, u32[]{:S(2)}, u32[]{:S(2)}) async-start(bf16[16,2,2560]{2,1,0:T(2,128)(2,1)} %reshape.335), calls=%async_computation | async-start | bytes 327680 | tf_op jit(solution)/shard_map/while/body/eval_jaxpr/all_to_all | solution.py:90
  66.9 0.7 copy-start.3
  67.7 10.8 %collective-permute-start = (bf16[32,5120]{1,0:T(8,128)(2,1)S(1)}, bf16[32,5120]{1,0:T(8,128)(2,1)S(1)}, u32[]{:S(2)}, u32[]{:S(2)}) collective-permute-start(bf16[32,5120]{1,0:T(8,128)(2,1)S(1)} %broadcast_select_fusion.3), channel_id=1, source_target_pairs={{0,16},{1,17},{2,18},{3,19},{4,20},{5,21},{6,22},{7,23},{8,24},{9,... | collective-permute-start | bytes 983048 | tf_op jit(solution)/shard_map/while/body/eval_jaxpr/ppermute | solution.py:36
  72.1 33.7 %copy-start.1 = (bf16[1,192,5120]{2,1,0:T(8,128)(2,1)S(1)}, bf16[1,192,5120]{2,1,0:T(8,128)(2,1)}, u32[]{:S(2)}) copy-start(bf16[1,192,5120]{2,1,0:T(8,128)(2,1)} %get-tuple-element.725) | copy-start | bytes 5898244 | tf_op jit(solution)/shard_map/while
  80.3 6.0 %collective-permute-start.1 = (bf16[1,1,1,5120]{3,0,2,1:T(2,128)(2,1)S(1)}, bf16[1,1,1,5120]{3,0,2,1:T(2,128)(2,1)S(1)}, u32[]{:S(2)}, u32[]{:S(2)}) collective-permute-start(bf16[1,1,1,5120]{3,0,2,1:T(2,128)(2,1)S(1)} %get-tuple-element.608), channel_id=1, source_target_pairs={{0,1},{1,2},{2,3},{3,4},{4,5},{5,6},{6,7},{7,8},{8,9},{9,10},{10,1... | collective-permute-start | bytes 30728 | tf_op jit(solution)/shard_map/while/body/eval_jaxpr/ppermute | solution.py:28
  80.4 6.8 %collective-permute-start.2 = (bf16[1,1,1,5120]{3,0,2,1:T(2,128)(2,1)S(1)}, bf16[1,1,1,5120]{3,0,2,1:T(2,128)(2,1)S(1)}, u32[]{:S(2)}, u32[]{:S(2)}) collective-permute-start(bf16[1,1,1,5120]{3,0,2,1:T(2,128)(2,1)S(1)} %get-tuple-element.609), channel_id=1, source_target_pairs={{0,2},{1,3},{2,4},{3,5},{4,6},{5,7},{6,8},{7,9},{8,10},{9,11},{10,... | collective-permute-start | bytes 30728 | tf_op jit(solution)/shard_map/while/body/eval_jaxpr/ppermute | solution.py:28
  81.1 8.6 %collective-permute-start.3 = (bf16[1,1,1,5120]{3,0,2,1:T(2,128)(2,1)S(1)}, bf16[1,1,1,5120]{3,0,2,1:T(2,128)(2,1)S(1)}, u32[]{:S(2)}, u32[]{:S(2)}) collective-permute-start(bf16[1,1,1,5120]{3,0,2,1:T(2,128)(2,1)S(1)} %get-tuple-element.610), channel_id=1, source_target_pairs={{0,3},{1,4},{2,5},{3,6},{4,7},{5,8},{6,9},{7,10},{8,11},{9,12},{10... | collective-permute-start | bytes 30728 | tf_op jit(solution)/shard_map/while/body/eval_jaxpr/ppermute | solution.py:28
  82.9 8.4 %collective-permute-start.4 = (bf16[1,1,1,5120]{3,0,2,1:T(2,128)(2,1)S(1)}, bf16[1,1,1,5120]{3,0,2,1:T(2,128)(2,1)S(1)}, u32[]{:S(2)}, u32[]{:S(2)}) collective-permute-start(bf16[1,1,1,5120]{3,0,2,1:T(2,128)(2,1)S(1)} %get-tuple-element.611), channel_id=1, source_target_pairs={{0,4},{1,5},{2,6},{3,7},{4,8},{5,9},{6,10},{7,11},{8,12},{9,13},{1... | collective-permute-start | bytes 30728 | tf_op jit(solution)/shard_map/while/body/eval_jaxpr/ppermute | solution.py:28
  83.5 7.8 %collective-permute-start.5 = (bf16[1,1,1,5120]{3,0,2,1:T(2,128)(2,1)S(1)}, bf16[1,1,1,5120]{3,0,2,1:T(2,128)(2,1)S(1)}, u32[]{:S(2)}, u32[]{:S(2)}) collective-permute-start(bf16[1,1,1,5120]{3,0,2,1:T(2,128)(2,1)S(1)} %get-tuple-element.612), channel_id=1, source_target_pairs={{0,5},{1,6},{2,7},{3,8},{4,9},{5,10},{6,11},{7,12},{8,13},{9,14},{... | collective-permute-start | bytes 30728 | tf_op jit(solution)/shard_map/while/body/eval_jaxpr/ppermute | solution.py:28
  86.3 6.9 %collective-permute-start.6 = (bf16[1,1,1,5120]{3,0,2,1:T(2,128)(2,1)S(1)}, bf16[1,1,1,5120]{3,0,2,1:T(2,128)(2,1)S(1)}, u32[]{:S(2)}, u32[]{:S(2)}) collective-permute-start(bf16[1,1,1,5120]{3,0,2,1:T(2,128)(2,1)S(1)} %get-tuple-element.613), channel_id=1, source_target_pairs={{0,6},{1,7},{2,8},{3,9},{4,10},{5,11},{6,12},{7,13},{8,14},{9,15},... | collective-permute-start | bytes 30728 | tf_op jit(solution)/shard_map/while/body/eval_jaxpr/ppermute | solution.py:28
  87.1 9.6 %collective-permute-start.7 = (bf16[1,1,1,5120]{3,0,2,1:T(2,128)(2,1)S(1)}, bf16[1,1,1,5120]{3,0,2,1:T(2,128)(2,1)S(1)}, u32[]{:S(2)}, u32[]{:S(2)}) collective-permute-start(bf16[1,1,1,5120]{3,0,2,1:T(2,128)(2,1)S(1)} %get-tuple-element.614), channel_id=1, source_target_pairs={{0,7},{1,8},{2,9},{3,10},{4,11},{5,12},{6,13},{7,14},{8,15},{9,0},... | collective-permute-start | bytes 30728 | tf_op jit(solution)/shard_map/while/body/eval_jaxpr/ppermute | solution.py:28
  89.7 7.1 %collective-permute-start.8 = (bf16[1,1,1,5120]{3,0,2,1:T(2,128)(2,1)S(1)}, bf16[1,1,1,5120]{3,0,2,1:T(2,128)(2,1)S(1)}, u32[]{:S(2)}, u32[]{:S(2)}) collective-permute-start(bf16[1,1,1,5120]{3,0,2,1:T(2,128)(2,1)S(1)} %get-tuple-element.615), channel_id=1, source_target_pairs={{0,8},{1,9},{2,10},{3,11},{4,12},{5,13},{6,14},{7,15},{8,0},{9,1},... | collective-permute-start | bytes 30728 | tf_op jit(solution)/shard_map/while/body/eval_jaxpr/ppermute | solution.py:28
  91.3 6.6 %collective-permute-start.9 = (bf16[1,1,1,5120]{3,0,2,1:T(2,128)(2,1)S(1)}, bf16[1,1,1,5120]{3,0,2,1:T(2,128)(2,1)S(1)}, u32[]{:S(2)}, u32[]{:S(2)}) collective-permute-start(bf16[1,1,1,5120]{3,0,2,1:T(2,128)(2,1)S(1)} %get-tuple-element.616), channel_id=1, source_target_pairs={{0,9},{1,10},{2,11},{3,12},{4,13},{5,14},{6,15},{7,0},{8,1},{9,2},... | collective-permute-start | bytes 30728 | tf_op jit(solution)/shard_map/while/body/eval_jaxpr/ppermute | solution.py:28
  91.3 8.1 %collective-permute-start.10 = (bf16[1,1,1,5120]{3,0,2,1:T(2,128)(2,1)S(1)}, bf16[1,1,1,5120]{3,0,2,1:T(2,128)(2,1)S(1)}, u32[]{:S(2)}, u32[]{:S(2)}) collective-permute-start(bf16[1,1,1,5120]{3,0,2,1:T(2,128)(2,1)S(1)} %get-tuple-element.617), channel_id=1, source_target_pairs={{0,10},{1,11},{2,12},{3,13},{4,14},{5,15},{6,0},{7,1},{8,2},{9,3},... | collective-permute-start | bytes 30728 | tf_op jit(solution)/shard_map/while/body/eval_jaxpr/ppermute | solution.py:28
  93.1 11.2 %collective-permute-start.11 = (bf16[1,1,1,5120]{3,0,2,1:T(2,128)(2,1)S(1)}, bf16[1,1,1,5120]{3,0,2,1:T(2,128)(2,1)S(1)}, u32[]{:S(2)}, u32[]{:S(2)}) collective-permute-start(bf16[1,1,1,5120]{3,0,2,1:T(2,128)(2,1)S(1)} %get-tuple-element.618), channel_id=1, source_target_pairs={{0,11},{1,12},{2,13},{3,14},{4,15},{5,0},{6,1},{7,2},{8,3},{9,4},{... | collective-permute-start | bytes 30728 | tf_op jit(solution)/shard_map/while/body/eval_jaxpr/ppermute | solution.py:28
  96.7 7.9 %collective-permute-start.12 = (bf16[1,1,1,5120]{3,0,2,1:T(2,128)(2,1)S(1)}, bf16[1,1,1,5120]{3,0,2,1:T(2,128)(2,1)S(1)}, u32[]{:S(2)}, u32[]{:S(2)}) collective-permute-start(bf16[1,1,1,5120]{3,0,2,1:T(2,128)(2,1)S(1)} %get-tuple-element.619), channel_id=1, source_target_pairs={{0,12},{1,13},{2,14},{3,15},{4,0},{5,1},{6,2},{7,3},{8,4},{9,5},{1... | collective-permute-start | bytes 30728 | tf_op jit(solution)/shard_map/while/body/eval_jaxpr/ppermute | solution.py:28
  96.8 8.1 %collective-permute-start.13 = (bf16[1,1,1,5120]{3,0,2,1:T(2,128)(2,1)S(1)}, bf16[1,1,1,5120]{3,0,2,1:T(2,128)(2,1)S(1)}, u32[]{:S(2)}, u32[]{:S(2)}) collective-permute-start(bf16[1,1,1,5120]{3,0,2,1:T(2,128)(2,1)S(1)} %get-tuple-element.620), channel_id=1, source_target_pairs={{0,13},{1,14},{2,15},{3,0},{4,1},{5,2},{6,3},{7,4},{8,5},{9,6},{10... | collective-permute-start | bytes 30728 | tf_op jit(solution)/shard_map/while/body/eval_jaxpr/ppermute | solution.py:28
  97.9 7.3 %collective-permute-start.14 = (bf16[1,1,1,5120]{3,0,2,1:T(2,128)(2,1)S(1)}, bf16[1,1,1,5120]{3,0,2,1:T(2,128)(2,1)S(1)}, u32[]{:S(2)}, u32[]{:S(2)}) collective-permute-start(bf16[1,1,1,5120]{3,0,2,1:T(2,128)(2,1)S(1)} %get-tuple-element.621), channel_id=1, source_target_pairs={{0,14},{1,15},{2,0},{3,1},{4,2},{5,3},{6,4},{7,5},{8,6},{9,7},{10,... | collective-permute-start | bytes 30728 | tf_op jit(solution)/shard_map/while/body/eval_jaxpr/ppermute | solution.py:28
  99.4 6.1 %collective-permute-start.15 = (bf16[1,1,1,5120]{3,0,2,1:T(2,128)(2,1)S(1)}, bf16[1,1,1,5120]{3,0,2,1:T(2,128)(2,1)S(1)}, u32[]{:S(2)}, u32[]{:S(2)}) collective-permute-start(bf16[1,1,1,5120]{3,0,2,1:T(2,128)(2,1)S(1)} %get-tuple-element.622), channel_id=1, source_target_pairs={{0,15},{1,0},{2,1},{3,2},{4,3},{5,4},{6,5},{7,6},{8,7},{9,8},{10,9... | collective-permute-start | bytes 30728 | tf_op jit(solution)/shard_map/while/body/eval_jaxpr/ppermute | solution.py:28
  105.8 8.5 %copy-start.4 = (bf16[1,5120,2]{1,2,0:T(2,128)(2,1)S(1)}, bf16[1,5120,2]{1,2,0:T(2,128)(2,1)}, u32[]{:S(2)}) copy-start(bf16[1,5120,2]{1,2,0:T(2,128)(2,1)} %get-tuple-element.722) | copy-start | bytes 61444 | tf_op jit(solution)/shard_map/while
  108.9 14.4 %copy-start.2 = (bf16[1,32,5120]{2,1,0:T(8,128)(2,1)S(1)}, bf16[1,32,5120]{2,1,0:T(8,128)(2,1)}, u32[]{:S(2)}) copy-start(bf16[1,32,5120]{2,1,0:T(8,128)(2,1)} %get-tuple-element.673) | copy-start | bytes 983044 | tf_op jit(solution)/shard_map/while
  110.7 11.9 %all-to-all-start = ((bf16[16,2,2560]{2,1,0:T(2,128)(2,1)}), bf16[16,2,2560]{2,1,0:T(2,128)(2,1)S(1)}, u32[]{:S(2)}, u32[]{:S(2)}) async-start(bf16[16,2,2560]{2,1,0:T(2,128)(2,1)} %reshape.335), calls=%async_computation | async-start | bytes 327680 | tf_op jit(solution)/shard_map/while/body/eval_jaxpr/all_to_all | solution.py:90
  124.2 0.7 copy-start.3
Sparse Core Ops, SparseCore 0:
  125.8 24.1 all-reduce.1
